TPU v7x, 32 devices: a whole 2x2x4 slice. The times are simulated.
32 devices in a mesh: group: 4 (over y, x), leaf: 8 (over z, core).
Axes of the slice: x: 2, y: 2, z: 4, core: 2. Of those that a mesh axis runs over, the one named last changes fastest.
Arguments:
- points: bfloat16 [65536, 64], P(('group', 'leaf')), may hold values from -1.1953125 to 1.1953125
- ordering: int32 [32, 2048], P(('group', 'leaf')), may hold values from 0 to 2047, each once within a row
- iterate: float32 [65536, 128], P(('group', 'leaf')), may hold values from -6 to 6
- target: float32 [65536, 128], P(('group', 'leaf')), may hold values from -18 to 18
- step_size: float32 [128], replicated, may hold values from 0.1 to 0.5
- leaf_basis: bfloat16 [65536, 256], P(('group', 'leaf')), may hold values from -0.125 to 0.125
- transfer: bfloat16 [32, 256, 256], P(('group', 'leaf')), may hold values from -0.375 to 0.375
- leaf_skeleton: bfloat16 [32, 256, 64], P(('group', 'leaf')), may hold values from -0.8984375 to 0.8984375
- cluster_skeleton: bfloat16 [4, 256, 64], P('group'), may hold values from -1.1953125 to 1.1953125
- near_table: int32 [32, 8], P(('group', 'leaf')), may hold values from 0 to 1, as said below
- far_table: int32 [32, 8], P(('group', 'leaf')), may hold values from 0 to 1, as said below
- cluster_far: int32 [4, 4], P('group'), may hold values from 0 to 1, as said below
Outputs:
- updated: float32 [65536, 128], P(('group', 'leaf'))
Inputs may be any that keep to these rules, and one draw needn't show every extreme that they name: `near_table`: entries 0 or 1; each leaf's own place is 1; a 1 stands only at places at most 3 away from the leaf's own place; each row has at most 7 ones, and some row exactly 7. `far_table`: entries 0 or 1, never 1 where near_table is 1. `cluster_far`: entries 0 or 1, zero on the diagonal. `ordering`: each row is a permutation.
All inputs are finite; a program needn't handle non-finite values.
Results may differ from a plain program's by a relative error of at most 0.0044.
Values may be sent and summed in bfloat16 or wider, within the bound.
No kernel may reach another device: no remote copies, remote signals or barrier semaphores. Data moves between devices by JAX's collectives and lax.ppermute only.
A program may use at most 128 MiB of HBM per device.

v0:
```python
import jax
import jax.numpy as jnp
from jax import lax
from jax.sharding import PartitionSpec as P

NEAR_MOST = 7


def passed_along(block, axis, distance):
    devices = range(lax.axis_size(axis))
    route = [(i - distance, i) for i in devices if i - distance in devices]
    return lax.ppermute(block, axis, route)


def kernel_tile(left, right):
    left_f = left.astype(jnp.float32)
    right_f = right.astype(jnp.float32)
    left_sq = jnp.sum(left_f * left_f, axis=1)
    right_sq = jnp.sum(right_f * right_f, axis=1)
    inner = lax.dot_general(
        left, right, (((1,), (1,)), ((), ())), preferred_element_type=jnp.float32
    )
    return jnp.exp(-(left_sq[:, None] + right_sq[None, :] - 2.0 * inner)).astype(jnp.bfloat16)


def body(
    points,
    ordering,
    iterate,
    target,
    step_size,
    leaf_basis,
    transfer,
    leaf_skeleton,
    cluster_skeleton,
    near_table,
    far_table,
    cluster_far,
):
    leaf_rows = points.shape[0]
    point_cols = points.shape[1]
    rhs_cols = iterate.shape[1]
    rank_cols = leaf_basis.shape[1]
    rounded = iterate.astype(jnp.bfloat16)
    coeffs = lax.dot_general(
        leaf_basis, rounded, (((0,), (0,)), ((), ())), preferred_element_type=jnp.float32
    ).astype(jnp.bfloat16)
    near_row = near_table[0]
    far_row = far_table[0]
    own_transfer = transfer[0]
    reach = (NEAR_MOST - 1) // 2
    joined = jnp.concatenate([points, rounded], axis=1)
    below_blocks = []
    above_blocks = []
    passing_below = joined
    passing_above = joined
    for distance in range(1, reach + 1):
        passing_below = passed_along(passing_below, "leaf", 1)
        passing_above = passed_along(passing_above, "leaf", -1)
        below_blocks.append(passing_below)
        above_blocks.append(passing_above)
    padded = jnp.concatenate(below_blocks[::-1] + [joined] + above_blocks, axis=0)
    myself = lax.axis_index("leaf")
    cluster_size = near_row.shape[0]

    def window_visit(position, summed):
        place = myself + position - reach
        inside = (place >= 0) & (place < cluster_size)
        listed = lax.dynamic_index_in_dim(
            near_row, jnp.clip(place, 0, cluster_size - 1), 0, keepdims=False
        )
        block = lax.dynamic_slice_in_dim(padded, position * leaf_rows, leaf_rows, 0)
        other_points = block[:, :point_cols]
        other_values = block[:, point_cols:]

        def include(current):
            return current + jnp.dot(
                kernel_tile(points, other_points), other_values, preferred_element_type=jnp.float32
            )

        return lax.cond(inside & (listed > 0), include, lambda current: current, summed)

    near_sum = lax.fori_loop(
        0, 2 * reach + 1, window_visit, jnp.zeros((leaf_rows, rhs_cols), jnp.float32)
    )

    def far_visit(skeletons, values):

        def visit(position, summed):
            listed = lax.dynamic_index_in_dim(far_row, position, 0, keepdims=False)

            def include(current):
                return current + jnp.dot(
                    kernel_tile(leaf_skeleton[0], skeletons[position]),
                    values[position],
                    preferred_element_type=jnp.float32,
                )

            return lax.cond(listed > 0, include, lambda current: current, summed)

        return visit

    empty_far = jnp.zeros((rank_cols, rhs_cols), jnp.float32)
    skeletons = lax.all_gather(leaf_skeleton, "leaf", axis=0, tiled=True)
    values = lax.all_gather(coeffs[None], "leaf", axis=0, tiled=True)
    far_sum = lax.fori_loop(0, skeletons.shape[0], far_visit(skeletons, values), empty_far)
    upward_terms = lax.dot_general(
        own_transfer, coeffs, (((0,), (0,)), ((), ())), preferred_element_type=jnp.float32
    )
    upper = lax.psum(upward_terms, "leaf").astype(jnp.bfloat16)
    cluster_row = cluster_far[0]
    skeletons = lax.all_gather(cluster_skeleton, "group", axis=0, tiled=True)
    values = lax.all_gather(upper[None], "group", axis=0, tiled=True)

    def visit(position, summed):
        listed = lax.dynamic_index_in_dim(cluster_row, position, 0, keepdims=False)

        def include(current):
            return current + jnp.dot(
                kernel_tile(cluster_skeleton[0], skeletons[position]),
                values[position],
                preferred_element_type=jnp.float32,
            )

        return lax.cond(listed > 0, include, lambda current: current, summed)

    lower = lax.fori_loop(0, skeletons.shape[0], visit, empty_far).astype(jnp.bfloat16)
    local = (far_sum + jnp.dot(own_transfer, lower, preferred_element_type=jnp.float32)).astype(
        jnp.bfloat16
    )
    image = jnp.dot(leaf_basis, local, preferred_element_type=jnp.float32) + near_sum
    sorted_target = target[ordering[0]]
    return iterate + step_size[None, :] * (sorted_target - image)


def solution(mesh):
    return jax.shard_map(
        body,
        mesh=mesh,
        in_specs=(
            P(("group", "leaf"), None),
            P(("group", "leaf"), None),
            P(("group", "leaf"), None),
            P(("group", "leaf"), None),
            P(),
            P(("group", "leaf"), None),
            P(("group", "leaf"), None, None),
            P(("group", "leaf"), None, None),
            P("group", None, None),
            P(("group", "leaf"), None),
            P(("group", "leaf"), None),
            P("group", None),
        ),
        out_specs=P(("group", "leaf"), None),
        check_vma=False,
    )
```

profile of v0, /device:TPU:15, one launch (start us, length us, event | category | flops | bytes accessed | tf_op | source)
XLA Modules:
  0.0 278.6 jit_solution(15546868874311557150)
XLA Ops:
  2.7 1.9 pad_maximum_fusion
  4.6 3.9 %collective-permute-start = (bf16[2048,192]{0,1:T(8,128)(2,1)}, bf16[2048,192]{0,1:T(8,128)(2,1)}, u32[]{:S(2)}, u32[]{:S(2)}) collective-permute-start(bf16[2048,192]{0,1:T(8,128)(2,1)} %pad_maximum_fusion), channel_id=1, source_target_pairs={{0,1},{1,2},{2,3},{3,4},{4,5},{5,6},{6,7},{8,9},{9,10},{10,11},{11... | collective-permute-start | bytes 2359304 | tf_op jit(solution)/shard_map/ppermute | solution.py:12
  8.5 1.9 collective-permute-start.3
  10.4 7.3 %collective-permute-done = bf16[2048,192]{0,1:T(8,128)(2,1)} collective-permute-done((bf16[2048,192]{0,1:T(8,128)(2,1)}, bf16[2048,192]{0,1:T(8,128)(2,1)}, u32[]{:S(2)}, u32[]{:S(2)}) %collective-permute-start) | collective-permute-done | bytes 786464 | tf_op jit(solution)/shard_map/ppermute | solution.py:12
  17.7 4.4 %collective-permute-start.1 = (bf16[2048,192]{0,1:T(8,128)(2,1)}, bf16[2048,192]{0,1:T(8,128)(2,1)}, u32[]{:S(2)}, u32[]{:S(2)}) collective-permute-start(bf16[2048,192]{0,1:T(8,128)(2,1)} %collective-permute-done), channel_id=1, source_target_pairs={{0,1},{1,2},{2,3},{3,4},{4,5},{5,6},{6,7},{8,9},{9,10},{10,11},{11... | collective-permute-start | bytes 2359304 | tf_op jit(solution)/shard_map/ppermute | solution.py:12
  22.8 25.1 %all-reduce.1 = bf16[256,128]{0,1:T(8,128)(2,1)S(1)} all-reduce(f32[256,128]{0,1:T(8,128)S(1)} %convolution_bitcast_fusion.2), channel_id=1, replica_groups=mesh['group'=4,'leaf'=8] {'leaf'}, use_global_device_ids=true, to_apply=%region_6.7 | all-reduce | flops 32768 | bytes 196608 | tf_op jit(solution)/shard_map/psum | solution.py:110
  47.9 17.8 %all-gather = bf16[2048,128]{1,0:T(8,128)(2,1)} all-gather(bf16[256,128]{1,0:T(8,128)(2,1)S(1)} %convolution_convert_fusion), channel_id=2, replica_groups=mesh['group'=4,'leaf'=8] {'leaf'}, dimensions={0}, use_global_device_ids=true | all-gather | bytes 589824 | tf_op jit(solution)/shard_map/all_gather | solution.py:105
  65.8 2.1 collective-permute-start.4
  67.8 4.1 %collective-permute-start.2 = (bf16[2048,192]{0,1:T(8,128)(2,1)}, bf16[2048,192]{0,1:T(8,128)(2,1)}, u32[]{:S(2)}, u32[]{:S(2)}) collective-permute-start(bf16[2048,192]{0,1:T(8,128)(2,1)} %collective-permute-done.1), channel_id=1, source_target_pairs={{0,1},{1,2},{2,3},{3,4},{4,5},{5,6},{6,7},{8,9},{9,10},{10,11},{11... | collective-permute-start | bytes 2359304 | tf_op jit(solution)/shard_map/ppermute | solution.py:12
  71.9 20.0 %all_gather.12 = bf16[8,256,64]{1,2,0:T(8,128)(2,1)} all-gather(bf16[1,256,64]{1,2,0:T(8,128)(2,1)S(1)} %copy-done.8), channel_id=1, replica_groups=mesh['group'=4,'leaf'=8] {'leaf'}, dimensions={0}, use_global_device_ids=true | all-gather | bytes 294912 | tf_op jit(solution)/shard_map/all_gather | solution.py:104
  93.1 1.9 copy.37
  95.7 17.8 %while.50 = (s32[]{:T(128)}, f32[256,128]{1,0:T(8,128)}, s32[8]{0:T(128)}, bf16[1,256,64]{2,1,0:T(8,128)(2,1)S(1)}, bf16[8,256,64]{2,1,0:T(8,128)(2,1)}, /*index...) while((s32[]{:T(128)}, f32[256,128]{1,0:T(8,128)}, s32[8]{0:T(128)}, bf16[1,256,64]{2,1,0:T(8,128)(2,1)S(1)}, ...), condition=%wide.region_5.6_spmd, body=%wide.region_0.5_spmd.sunk | while | flops 25624072 | bytes 496837 | solution.py:106
  110.4 3.1 %conditional.6 = (f32[256,128]{1,0:T(8,128)}) conditional(s32[]{:T(128)} %bitcast.109, f32[256,128]{1,0:T(8,128)} %get-tuple-element.740, (bf16[1,256,64]{2,1,0:T(8,128)(2,1)S(1)}, s32[]{:T(128)}, bf16[8,256,64]{2,1,0:T(8,128)(2,1)}, bf16[8,256,128]{2,1,0:T(8,128)(2,1)}, f32[256,128]{1,0:T(8,128)}) %tuple.135), branch_computations={%region_1.1_spmd, %region_2.4_spmd} | conditional | flops 25624068 | bytes 496686 | solution.py:99
  111.4 2.1 fusion.6
  115.2 13.8 %all-gather.1 = bf16[1024,128]{0,1:T(8,128)(2,1)} all-gather(bf16[256,128]{0,1:T(8,128)(2,1)S(1)} %all-reduce.1), channel_id=3, replica_groups=mesh['group'=4,'leaf'=8] {'group'}, dimensions={0}, use_global_device_ids=true | all-gather | bytes 327680 | tf_op jit(solution)/shard_map/all_gather | solution.py:113
  128.9 1.8 copy.48
  131.6 7.2 %all_gather.14 = bf16[4,256,64]{1,2,0:T(8,128)(2,1)} all-gather(bf16[1,256,64]{1,2,0:T(8,128)(2,1)} %param.32), channel_id=1, replica_groups=mesh['group'=4,'leaf'=8] {'group'}, dimensions={0}, use_global_device_ids=true | all-gather | bytes 163840 | tf_op jit(solution)/shard_map/all_gather | solution.py:112
  138.8 1.8 copy.39
  140.6 7.6 %gather_fusion = f32[2048,128]{1,0:T(8,128)} fusion(f32[2048,128]{1,0:T(8,128)S(1)} %copy-done.1, s32[2048]{0:T(1024)S(1)} %broadcast_clamp_fusion), kind=kCustom, calls=%fused_computation | custom fusion | bytes 2105344 | tf_op jit(solution)/shard_map/gather | solution.py:132
  148.2 2.6 copy.45
  150.8 9.8 %while.51 = (s32[]{:T(128)}, f32[256,128]{1,0:T(8,128)S(1)}, s32[4]{0:T(128)S(1)}, bf16[1,256,64]{2,1,0:T(8,128)(2,1)S(1)}, bf16[4,256,64]{2,1,0:T(8,128)(2,1)},...) while((s32[]{:T(128)}, f32[256,128]{1,0:T(8,128)S(1)}, s32[4]{0:T(128)S(1)}, ...), condition=%wide.region_12.13_spmd, body=%wide.region_7.12_spmd.sunk | while | flops 25624072 | bytes 496837 | solution.py:127
  153.4 2.3 conditional.7
  157.0 2.3 conditional.7
  160.7 9.4 %collective-permute-start.5 = (bf16[2048,192]{0,1:T(8,128)(2,1)}, bf16[2048,192]{0,1:T(8,128)(2,1)S(1)}, u32[]{:S(2)}, u32[]{:S(2)}) collective-permute-start(bf16[2048,192]{0,1:T(8,128)(2,1)} %collective-permute-done.4), channel_id=1, source_target_pairs={{1,0},{2,1},{3,2},{4,3},{5,4},{6,5},{7,6},{9,8},{10,9},{11,10},{12... | collective-permute-start | bytes 2359304 | tf_op jit(solution)/shard_map/ppermute | solution.py:12
  170.1 2.2 constant_dynamic-update-slice_fusion.6
  172.3 2.1 constant_dynamic-update-slice_fusion.5
  174.4 2.2 constant_dynamic-update-slice_fusion.4
  177.5 2.2 constant_dynamic-update-slice_fusion.2
  179.7 2.2 constant_dynamic-update-slice_fusion.1
  182.8 9.2 %copy.43 = bf16[14336,192]{1,0:T(8,128)(2,1)} copy(bf16[14336,192]{0,1:T(8,128)(2,1)} %constant_dynamic-update-slice_fusion) | data formatting | bytes 11010048 | tf_op jit(solution)/shard_map/while | solution.py:83
  193.2 77.1 %while.52 = (s32[]{:T(128)}, f32[2048,128]{1,0:T(8,128)}, s32[]{:T(128)}, s32[8]{0:T(128)S(1)}, bf16[2048,64]{1,0:T(8,128)(2,1)S(1)}, /*index=5*/bf16[14336,192]...) while((s32[]{:T(128)}, f32[2048,128]{1,0:T(8,128)}, ...), condition=%wide.region_18.19_spmd, body=%wide.region_13.18_spmd.sunk | while | flops 1632628736 | bytes 3966781 | solution.py:83
  194.5 9.7 %conditional.8 = (f32[2048,128]{1,0:T(8,128)}) conditional(s32[]{:T(128)} %convert_element_type.116, f32[2048,128]{1,0:T(8,128)} %get-tuple-element.708, (bf16[2048,64]{1,0:T(8,128)(2,1)S(1)}, s32[]{:T(128)}, bf16[14336,192]{1,0:T(8,128)(2,1)}, f32[2048,128]{1,0:T(8,128)}) %tuple.139), branch_computations={%region_14.14_spmd, %region_15.17_spmd} | conditional | flops 1632628736 | bytes 3966534 | solution.py:81
  196.2 8.0 %convolution_add_fusion = f32[2048,128]{1,0:T(8,128)} fusion(f32[2048,128]{1,0:T(8,128)} %get-tuple-element.471, bf16[2048,64]{1,0:T(8,128)(2,1)S(1)} %get-tuple-element.472, f32[2048]{0:T(1024)S(1)} %get-tuple-element.582, f32[2048]{0:T(1024)S(1)} %get-tuple-element.583, bf16[14336,192]{1,0:T(8,128)(2,1)} %get-tuple-element.473, s32[]{:T(128)S(6)} %select_n.45, ...), kind=kOutput, calls=%fused_computation.47 | convolution fusion | flops 1631846400 | bytes 3425792 | tf_op jit(solution)/shard_map/while/body/eval_jaxpr/cond/branch_1_fun/dot_general | solution.py:77
  205.5 9.7 %conditional.8 = (f32[2048,128]{1,0:T(8,128)}) conditional(s32[]{:T(128)} %convert_element_type.116, f32[2048,128]{1,0:T(8,128)} %get-tuple-element.708, (bf16[2048,64]{1,0:T(8,128)(2,1)S(1)}, s32[]{:T(128)}, bf16[14336,192]{1,0:T(8,128)(2,1)}, f32[2048,128]{1,0:T(8,128)}) %tuple.139), branch_computations={%region_14.14_spmd, %region_15.17_spmd} | conditional | flops 1632628736 | bytes 3966534 | solution.py:81
  207.2 8.0 %convolution_add_fusion = f32[2048,128]{1,0:T(8,128)} fusion(f32[2048,128]{1,0:T(8,128)} %get-tuple-element.471, bf16[2048,64]{1,0:T(8,128)(2,1)S(1)} %get-tuple-element.472, f32[2048]{0:T(1024)S(1)} %get-tuple-element.582, f32[2048]{0:T(1024)S(1)} %get-tuple-element.583, bf16[14336,192]{1,0:T(8,128)(2,1)} %get-tuple-element.473, s32[]{:T(128)S(6)} %select_n.45, ...), kind=kOutput, calls=%fused_computation.47 | convolution fusion | flops 1631846400 | bytes 3425792 | tf_op jit(solution)/shard_map/while/body/eval_jaxpr/cond/branch_1_fun/dot_general | solution.py:77
  216.5 9.7 %conditional.8 = (f32[2048,128]{1,0:T(8,128)}) conditional(s32[]{:T(128)} %convert_element_type.116, f32[2048,128]{1,0:T(8,128)} %get-tuple-element.708, (bf16[2048,64]{1,0:T(8,128)(2,1)S(1)}, s32[]{:T(128)}, bf16[14336,192]{1,0:T(8,128)(2,1)}, f32[2048,128]{1,0:T(8,128)}) %tuple.139), branch_computations={%region_14.14_spmd, %region_15.17_spmd} | conditional | flops 1632628736 | bytes 3966534 | solution.py:81
  218.2 8.0 %convolution_add_fusion = f32[2048,128]{1,0:T(8,128)} fusion(f32[2048,128]{1,0:T(8,128)} %get-tuple-element.471, bf16[2048,64]{1,0:T(8,128)(2,1)S(1)} %get-tuple-element.472, f32[2048]{0:T(1024)S(1)} %get-tuple-element.582, f32[2048]{0:T(1024)S(1)} %get-tuple-element.583, bf16[14336,192]{1,0:T(8,128)(2,1)} %get-tuple-element.473, s32[]{:T(128)S(6)} %select_n.45, ...), kind=kOutput, calls=%fused_computation.47 | convolution fusion | flops 1631846400 | bytes 3425792 | tf_op jit(solution)/shard_map/while/body/eval_jaxpr/cond/branch_1_fun/dot_general | solution.py:77
  227.5 9.7 %conditional.8 = (f32[2048,128]{1,0:T(8,128)}) conditional(s32[]{:T(128)} %convert_element_type.116, f32[2048,128]{1,0:T(8,128)} %get-tuple-element.708, (bf16[2048,64]{1,0:T(8,128)(2,1)S(1)}, s32[]{:T(128)}, bf16[14336,192]{1,0:T(8,128)(2,1)}, f32[2048,128]{1,0:T(8,128)}) %tuple.139), branch_computations={%region_14.14_spmd, %region_15.17_spmd} | conditional | flops 1632628736 | bytes 3966534 | solution.py:81
  229.2 8.0 %convolution_add_fusion = f32[2048,128]{1,0:T(8,128)} fusion(f32[2048,128]{1,0:T(8,128)} %get-tuple-element.471, bf16[2048,64]{1,0:T(8,128)(2,1)S(1)} %get-tuple-element.472, f32[2048]{0:T(1024)S(1)} %get-tuple-element.582, f32[2048]{0:T(1024)S(1)} %get-tuple-element.583, bf16[14336,192]{1,0:T(8,128)(2,1)} %get-tuple-element.473, s32[]{:T(128)S(6)} %select_n.45, ...), kind=kOutput, calls=%fused_computation.47 | convolution fusion | flops 1631846400 | bytes 3425792 | tf_op jit(solution)/shard_map/while/body/eval_jaxpr/cond/branch_1_fun/dot_general | solution.py:77
  238.5 9.7 %conditional.8 = (f32[2048,128]{1,0:T(8,128)}) conditional(s32[]{:T(128)} %convert_element_type.116, f32[2048,128]{1,0:T(8,128)} %get-tuple-element.708, (bf16[2048,64]{1,0:T(8,128)(2,1)S(1)}, s32[]{:T(128)}, bf16[14336,192]{1,0:T(8,128)(2,1)}, f32[2048,128]{1,0:T(8,128)}) %tuple.139), branch_computations={%region_14.14_spmd, %region_15.17_spmd} | conditional | flops 1632628736 | bytes 3966534 | solution.py:81
  240.2 8.0 %convolution_add_fusion = f32[2048,128]{1,0:T(8,128)} fusion(f32[2048,128]{1,0:T(8,128)} %get-tuple-element.471, bf16[2048,64]{1,0:T(8,128)(2,1)S(1)} %get-tuple-element.472, f32[2048]{0:T(1024)S(1)} %get-tuple-element.582, f32[2048]{0:T(1024)S(1)} %get-tuple-element.583, bf16[14336,192]{1,0:T(8,128)(2,1)} %get-tuple-element.473, s32[]{:T(128)S(6)} %select_n.45, ...), kind=kOutput, calls=%fused_computation.47 | convolution fusion | flops 1631846400 | bytes 3425792 | tf_op jit(solution)/shard_map/while/body/eval_jaxpr/cond/branch_1_fun/dot_general | solution.py:77
  249.5 9.7 %conditional.8 = (f32[2048,128]{1,0:T(8,128)}) conditional(s32[]{:T(128)} %convert_element_type.116, f32[2048,128]{1,0:T(8,128)} %get-tuple-element.708, (bf16[2048,64]{1,0:T(8,128)(2,1)S(1)}, s32[]{:T(128)}, bf16[14336,192]{1,0:T(8,128)(2,1)}, f32[2048,128]{1,0:T(8,128)}) %tuple.139), branch_computations={%region_14.14_spmd, %region_15.17_spmd} | conditional | flops 1632628736 | bytes 3966534 | solution.py:81
  251.2 8.1 %convolution_add_fusion = f32[2048,128]{1,0:T(8,128)} fusion(f32[2048,128]{1,0:T(8,128)} %get-tuple-element.471, bf16[2048,64]{1,0:T(8,128)(2,1)S(1)} %get-tuple-element.472, f32[2048]{0:T(1024)S(1)} %get-tuple-element.582, f32[2048]{0:T(1024)S(1)} %get-tuple-element.583, bf16[14336,192]{1,0:T(8,128)(2,1)} %get-tuple-element.473, s32[]{:T(128)S(6)} %select_n.45, ...), kind=kOutput, calls=%fused_computation.47 | convolution fusion | flops 1631846400 | bytes 3425792 | tf_op jit(solution)/shard_map/while/body/eval_jaxpr/cond/branch_1_fun/dot_general | solution.py:77
  260.5 9.8 %conditional.8 = (f32[2048,128]{1,0:T(8,128)}) conditional(s32[]{:T(128)} %convert_element_type.116, f32[2048,128]{1,0:T(8,128)} %get-tuple-element.708, (bf16[2048,64]{1,0:T(8,128)(2,1)S(1)}, s32[]{:T(128)}, bf16[14336,192]{1,0:T(8,128)(2,1)}, f32[2048,128]{1,0:T(8,128)}) %tuple.139), branch_computations={%region_14.14_spmd, %region_15.17_spmd} | conditional | flops 1632628736 | bytes 3966534 | solution.py:81
  262.2 8.1 %convolution_add_fusion = f32[2048,128]{1,0:T(8,128)} fusion(f32[2048,128]{1,0:T(8,128)} %get-tuple-element.471, bf16[2048,64]{1,0:T(8,128)(2,1)S(1)} %get-tuple-element.472, f32[2048]{0:T(1024)S(1)} %get-tuple-element.582, f32[2048]{0:T(1024)S(1)} %get-tuple-element.583, bf16[14336,192]{1,0:T(8,128)(2,1)} %get-tuple-element.473, s32[]{:T(128)S(6)} %select_n.45, ...), kind=kOutput, calls=%fused_computation.47 | convolution fusion | flops 1631846400 | bytes 3425792 | tf_op jit(solution)/shard_map/while/body/eval_jaxpr/cond/branch_1_fun/dot_general | solution.py:77
  270.3 2.5 copy.44
  272.9 3.2 %fusion.56 = f32[2048,128]{0,1:T(8,128)} fusion(f32[2048,128]{0,1:T(8,128)S(1)} %copy-done.3, f32[2048,128]{0,1:T(8,128)} %copy.45, f32[2048,128]{0,1:T(8,128)} %copy.44, bf16[2048,256]{1,0:T(8,128)(2,1)S(1)} %copy-done, f32[256,128]{0,1:T(8,128)S(1)} %copy-done.7, f32[128]{0:T(128)S(1)} %copy-done.10, bf16[1,256,256]{2,1,0:T(8,128)(2,1)S(1)} %copy-done.6, ...), kind=kOutput, calls=%fused_computation.58 | convolution fusion | flops 152141824 | bytes 5636608 | tf_op jit(solution)/shard_map/dot_general | solution.py:131
  276.1 2.5 copy.47
  (86 shorter events, 44.8 us)
Async XLA Ops:
  0.0 22.1 %copy-start = (bf16[2048,256]{1,0:T(8,128)(2,1)S(1)}, bf16[2048,256]{1,0:T(8,128)(2,1)}, u32[]{:S(2)}) copy-start(bf16[2048,256]{1,0:T(8,128)(2,1)} %param.29) | copy-start | bytes 3145732
  0.0 91.9 %copy-start.4 = (bf16[2048,64]{0,1:T(8,128)(2,1)S(1)}, bf16[2048,64]{0,1:T(8,128)(2,1)}, u32[]{:S(2)}) copy-start(bf16[2048,64]{0,1:T(8,128)(2,1)} %param.24) | copy-start | bytes 786436
  0.0 22.6 %copy-start.5 = (bf16[1,256,256]{2,1,0:T(8,128)(2,1)S(1)}, bf16[1,256,256]{2,1,0:T(8,128)(2,1)}, u32[]{:S(2)}) copy-start(bf16[1,256,256]{2,1,0:T(8,128)(2,1)} %param.30) | copy-start | bytes 393220
  0.0 71.9 %copy-start.8 = (bf16[1,256,64]{1,2,0:T(8,128)(2,1)S(1)}, bf16[1,256,64]{1,2,0:T(8,128)(2,1)}, u32[]{:S(2)}) copy-start(bf16[1,256,64]{1,2,0:T(8,128)(2,1)} %param.31) | copy-start | bytes 98308
  1.7 1.0 copy-start.2
  2.7 137.9 %copy-start.9 = (s32[1,2048]{1,0:T(1,128)S(1)}, s32[1,2048]{1,0:T(1,128)}, u32[]{:S(2)}) copy-start(s32[1,2048]{1,0:T(1,128)} %param.25) | copy-start | bytes 24580
  4.6 136.0 %copy-start.1 = (f32[2048,128]{1,0:T(8,128)S(1)}, f32[2048,128]{1,0:T(8,128)}, u32[]{:S(2)}) copy-start(f32[2048,128]{1,0:T(8,128)} %param.27) | copy-start | bytes 3145732
  4.6 13.1 %collective-permute-start = (bf16[2048,192]{0,1:T(8,128)(2,1)}, bf16[2048,192]{0,1:T(8,128)(2,1)}, u32[]{:S(2)}, u32[]{:S(2)}) collective-permute-start(bf16[2048,192]{0,1:T(8,128)(2,1)} %pad_maximum_fusion), channel_id=1, source_target_pairs={{0,1},{1,2},{2,3},{3,4},{4,5},{5,6},{6,7},{8,9},{9,10},{10,11},{11... | collective-permute-start | bytes 2359304 | tf_op jit(solution)/shard_map/ppermute | solution.py:12
  8.5 57.3 %collective-permute-start.3 = (bf16[2048,192]{0,1:T(8,128)(2,1)}, bf16[2048,192]{0,1:T(8,128)(2,1)}, u32[]{:S(2)}, u32[]{:S(2)}) collective-permute-start(bf16[2048,192]{0,1:T(8,128)(2,1)} %pad_maximum_fusion), channel_id=1, source_target_pairs={{1,0},{2,1},{3,2},{4,3},{5,4},{6,5},{7,6},{9,8},{10,9},{11,10},{12... | collective-permute-start | bytes 2359304 | tf_op jit(solution)/shard_map/ppermute | solution.py:12
  17.7 50.1 %collective-permute-start.1 = (bf16[2048,192]{0,1:T(8,128)(2,1)}, bf16[2048,192]{0,1:T(8,128)(2,1)}, u32[]{:S(2)}, u32[]{:S(2)}) collective-permute-start(bf16[2048,192]{0,1:T(8,128)(2,1)} %collective-permute-done), channel_id=1, source_target_pairs={{0,1},{1,2},{2,3},{3,4},{4,5},{5,6},{6,7},{8,9},{9,10},{10,11},{11... | collective-permute-start | bytes 2359304 | tf_op jit(solution)/shard_map/ppermute | solution.py:12
  65.8 94.9 %collective-permute-start.4 = (bf16[2048,192]{0,1:T(8,128)(2,1)}, bf16[2048,192]{0,1:T(8,128)(2,1)}, u32[]{:S(2)}, u32[]{:S(2)}) collective-permute-start(bf16[2048,192]{0,1:T(8,128)(2,1)} %collective-permute-done.3), channel_id=1, source_target_pairs={{1,0},{2,1},{3,2},{4,3},{5,4},{6,5},{7,6},{9,8},{10,9},{11,10},{12... | collective-permute-start | bytes 2359304 | tf_op jit(solution)/shard_map/ppermute | solution.py:12
  67.8 102.2 %collective-permute-start.2 = (bf16[2048,192]{0,1:T(8,128)(2,1)}, bf16[2048,192]{0,1:T(8,128)(2,1)}, u32[]{:S(2)}, u32[]{:S(2)}) collective-permute-start(bf16[2048,192]{0,1:T(8,128)(2,1)} %collective-permute-done.1), channel_id=1, source_target_pairs={{0,1},{1,2},{2,3},{3,4},{4,5},{5,6},{6,7},{8,9},{9,10},{10,11},{11... | collective-permute-start | bytes 2359304 | tf_op jit(solution)/shard_map/ppermute | solution.py:12
  140.6 10.2 %copy-start.11 = (s32[1,4]{1,0:T(1,128)S(1)}, s32[1,4]{1,0:T(1,128)}, u32[]{:S(2)}) copy-start(s32[1,4]{1,0:T(1,128)} %param.35) | copy-start | bytes 52
  160.7 21.2 %collective-permute-start.5 = (bf16[2048,192]{0,1:T(8,128)(2,1)}, bf16[2048,192]{0,1:T(8,128)(2,1)S(1)}, u32[]{:S(2)}, u32[]{:S(2)}) collective-permute-start(bf16[2048,192]{0,1:T(8,128)(2,1)} %collective-permute-done.4), channel_id=1, source_target_pairs={{1,0},{2,1},{3,2},{4,3},{5,4},{6,5},{7,6},{9,8},{10,9},{11,10},{12... | collective-permute-start | bytes 2359304 | tf_op jit(solution)/shard_map/ppermute | solution.py:12
  182.8 10.3 %copy-start.12 = (s32[1,8]{1,0:T(1,128)S(1)}, s32[1,8]{1,0:T(1,128)}, u32[]{:S(2)}) copy-start(s32[1,8]{1,0:T(1,128)} %param.33) | copy-start | bytes 100
  193.1 79.7 %copy-start.3 = (f32[2048,128]{0,1:T(8,128)S(1)}, f32[2048,128]{0,1:T(8,128)}, u32[]{:S(2)}) copy-start(f32[2048,128]{0,1:T(8,128)} %copy-done.2) | copy-start | bytes 3145732
  193.1 79.7 %copy-start.6 = (bf16[1,256,256]{2,1,0:T(8,128)(2,1)S(1)}, bf16[1,256,256]{2,1,0:T(8,128)(2,1)}, u32[]{:S(2)}) copy-start(bf16[1,256,256]{2,1,0:T(8,128)(2,1)} %param.30) | copy-start | bytes 393220
  193.1 79.7 %copy-start.7 = (f32[256,128]{0,1:T(8,128)S(1)}, f32[256,128]{0,1:T(8,128)}, u32[]{:S(2)}) copy-start(f32[256,128]{0,1:T(8,128)} %copy.41) | copy-start | bytes 393220
  193.2 79.7 %copy-start.10 = (f32[128]{0:T(128)S(1)}, f32[128]{0:T(128)}, u32[]{:S(2)}) copy-start(f32[128]{0:T(128)} %param.28) | copy-start | bytes 1540
where the time goes:
time: 281 us; the launch traced here: 279 us
  blocking collectives  84 us (30%)
  local copies, waits for them, and re-layouts  66.5 us (24%)
  matrix products  65 us (23%)
  starting transfers between devices  25.7 us (9%)
  other arithmetic  17.5 us (6%)
  loops' own time  12.3 us (4%)
  waiting for transfers between devices  7.31 us (3%)
    dot_general x7, matrix products, include(): jnp.dot(kernel_tile(points, other_points), other_values, preferred_elemen...  56.4 us
    ppermute x6, starting transfers between devices, passed_along(): return lax.ppermute(block, axis, route)  25.7 us
    psum x1, blocking collectives, body(): upper = lax.psum(upward_terms, 'leaf').astype(jnp.bfloat16)  25.1 us
    all_gather x1, blocking collectives, body(): skeletons = lax.all_gather(leaf_skeleton, 'leaf', axis=0, tiled=True)  20 us
    all_gather x1, blocking collectives, body(): values = lax.all_gather(coeffs[None], 'leaf', axis=0, tiled=True)  17.8 us
    reduce_sum x10, other arithmetic, kernel_tile(): right_sq = jnp.sum(right_f * right_f, axis=1)  14.6 us
    all_gather x1, blocking collectives, body(): values = lax.all_gather(upper[None], 'group', axis=0, tiled=True)  13.8 us
    unnamed x32, local copies, waits for them, and re-layouts  13.4 us
  transfers between devices with their start and end apart: 6, of which 1 were waited for; matrix products, arithmetic and copies ran while one was open for 19% of the time, Pallas kernels for 0%

commit v1 on v0

--- a/solution.py
+++ b/solution.py
@@ -110,7 +110,14 @@
     upper = lax.psum(upward_terms, "leaf").astype(jnp.bfloat16)
     cluster_row = cluster_far[0]
     skeletons = lax.all_gather(cluster_skeleton, "group", axis=0, tiled=True)
-    values = lax.all_gather(upper[None], "group", axis=0, tiled=True)
+    ring = [upper[None]]
+    for hop in range(3):
+        ring.append(lax.ppermute(ring[-1], "group", [(dev, (dev + 1) % 4) for dev in range(4)]))
+    values = jnp.roll(
+        jnp.concatenate(ring[::-1], axis=0),
+        (lax.axis_index("group") + 1) * ring[0].shape[0],
+        axis=0,
+    )
 
     def visit(position, summed):
         listed = lax.dynamic_index_in_dim(cluster_row, position, 0, keepdims=False)

time: 281 us -> 270 us (0.961)
  blocking collectives: 84 us -> 71.5 us
  waiting for transfers between devices: 7.31 us -> 2.13 us
  starting transfers between devices: 25.7 us -> 30.7 us
    all_gather x1 -> x0, blocking collectives: 13.8 us -> none  [body(): values = lax.all_gather(upper[None], 'group', axis=0, tiled=True)]
    ppermute x6, waiting for transfers between devices: 7.31 us -> 0.12 us  [passed_along(): return lax.ppermute(block, axis, route)]
    unnamed x32 -> x49, local copies, waits for them, and re-layouts: 13.4 us -> 17.3 us
    ppermute x0 -> x3, starting transfers between devices: none -> 3.57 us  [body(): lax.ppermute(ring[-1], 'group', [(dev, (dev + 1) % 4) for dev in range(4)])]
    all_gather x1, blocking collectives: 20 us -> 17 us  [body(): skeletons = lax.all_gather(leaf_skeleton, 'leaf', axis=0, tiled=True)]
  transfers between devices with their start and end apart: 6 -> 9, of which waited for: 1 -> 2; matrix products, arithmetic and copies ran while one was open for 19% -> 21% of each run, Pallas kernels for 0% -> 0%
where the time goes in v1:
time: 270 us; the launch traced here: 267 us
  blocking collectives  71.5 us (26%)
  local copies, waits for them, and re-layouts  68.2 us (25%)
  matrix products  64.7 us (24%)
  starting transfers between devices  30.7 us (11%)
  other arithmetic  17.7 us (7%)
  loops' own time  12 us (4%)
    dot_general x7, matrix products, include(): jnp.dot(kernel_tile(points, other_points), other_values, preferred_elemen...  56.4 us
    ppermute x6, starting transfers between devices, passed_along(): return lax.ppermute(block, axis, route)  27.1 us
    psum x1, blocking collectives, body(): upper = lax.psum(upward_terms, 'leaf').astype(jnp.bfloat16)  26.7 us
    all_gather x1, blocking collectives, body(): values = lax.all_gather(coeffs[None], 'leaf', axis=0, tiled=True)  20.6 us
    unnamed x49, local copies, waits for them, and re-layouts  17.3 us
    all_gather x1, blocking collectives, body(): skeletons = lax.all_gather(leaf_skeleton, 'leaf', axis=0, tiled=True)  17 us
    reduce_sum x10, other arithmetic, kernel_tile(): right_sq = jnp.sum(right_f * right_f, axis=1)  14.6 us
    while x3, local copies, waits for them, and re-layouts, body(): lax.fori_loop(0, 2 * reach + 1, window_visit, jnp.zeros((leaf_rows, rhs_c...  11.1 us
  transfers between devices with their start and end apart: 9, of which 2 were waited for; matrix products, arithmetic and copies ran while one was open for 21% of the time, Pallas kernels for 0%

profile of v1, /device:TPU:15, one launch (start us, length us, event | category | flops | bytes accessed | tf_op | source)
XLA Modules:
  0.0 267.4 jit_solution(8949136111322257390)
XLA Ops:
  0.0 1.7 copy.46
  2.8 2.0 pad_maximum_fusion
  4.8 3.8 %collective-permute-start.3 = (bf16[2048,192]{0,1:T(8,128)(2,1)}, bf16[2048,192]{0,1:T(8,128)(2,1)}, u32[]{:S(2)}, u32[]{:S(2)}) collective-permute-start(bf16[2048,192]{0,1:T(8,128)(2,1)} %pad_maximum_fusion), channel_id=1, source_target_pairs={{0,1},{1,2},{2,3},{3,4},{4,5},{5,6},{6,7},{8,9},{9,10},{10,11},{11... | collective-permute-start | bytes 2359304 | tf_op jit(solution)/shard_map/ppermute | solution.py:12
  8.5 1.9 collective-permute-start.6
  11.1 26.7 %all-reduce.1 = bf16[256,128]{0,1:T(8,128)(2,1)S(1)} all-reduce(f32[256,128]{0,1:T(8,128)S(1)} %convolution_bitcast_fusion.2), channel_id=1, replica_groups=mesh['group'=4,'leaf'=8] {'leaf'}, use_global_device_ids=true, to_apply=%region_6.7 | all-reduce | flops 32768 | bytes 196608 | tf_op jit(solution)/shard_map/psum | solution.py:110
  38.2 3.8 %collective-permute-start.4 = (bf16[2048,192]{0,1:T(8,128)(2,1)}, bf16[2048,192]{0,1:T(8,128)(2,1)}, u32[]{:S(2)}, u32[]{:S(2)}) collective-permute-start(bf16[2048,192]{0,1:T(8,128)(2,1)} %collective-permute-done.3), channel_id=1, source_target_pairs={{0,1},{1,2},{2,3},{3,4},{4,5},{5,6},{6,7},{8,9},{9,10},{10,11},{11... | collective-permute-start | bytes 2359304 | tf_op jit(solution)/shard_map/ppermute | solution.py:12
  42.0 20.6 %all-gather = bf16[2048,128]{1,0:T(8,128)(2,1)} all-gather(bf16[256,128]{1,0:T(8,128)(2,1)S(1)} %convolution_convert_fusion), channel_id=2, replica_groups=mesh['group'=4,'leaf'=8] {'leaf'}, dimensions={0}, use_global_device_ids=true | all-gather | bytes 589824 | tf_op jit(solution)/shard_map/all_gather | solution.py:105
  63.8 2.0 collective-permute-done.1
  65.8 2.1 collective-permute-start.2
  67.9 17.0 %all_gather.9 = bf16[8,256,64]{1,2,0:T(8,128)(2,1)} all-gather(bf16[1,256,64]{1,2,0:T(8,128)(2,1)S(1)} %copy-done.13), channel_id=1, replica_groups=mesh['group'=4,'leaf'=8] {'leaf'}, dimensions={0}, use_global_device_ids=true | all-gather | bytes 294912 | tf_op jit(solution)/shard_map/all_gather | solution.py:104
  86.9 7.2 %all_gather.11 = bf16[4,256,64]{1,2,0:T(8,128)(2,1)} all-gather(bf16[1,256,64]{1,2,0:T(8,128)(2,1)} %param.32), channel_id=1, replica_groups=mesh['group'=4,'leaf'=8] {'group'}, dimensions={0}, use_global_device_ids=true | all-gather | bytes 163840 | tf_op jit(solution)/shard_map/all_gather | solution.py:112
  94.1 1.8 copy.39
  95.9 2.0 copy.37
  98.5 18.6 %while.50 = (s32[]{:T(128)}, f32[256,128]{1,0:T(8,128)}, s32[8]{0:T(128)}, bf16[1,256,64]{2,1,0:T(8,128)(2,1)S(1)}, bf16[8,256,64]{2,1,0:T(8,128)(2,1)}, /*index...) while((s32[]{:T(128)}, f32[256,128]{1,0:T(8,128)}, s32[8]{0:T(128)}, bf16[1,256,64]{2,1,0:T(8,128)(2,1)S(1)}, ...), condition=%wide.region_5.6_spmd, body=%wide.region_0.5_spmd.sunk | while | flops 25624072 | bytes 496837 | solution.py:106
  114.0 3.1 %conditional.6 = (f32[256,128]{1,0:T(8,128)}) conditional(s32[]{:T(128)} %bitcast.113, f32[256,128]{1,0:T(8,128)} %get-tuple-element.740, (bf16[1,256,64]{2,1,0:T(8,128)(2,1)S(1)}, s32[]{:T(128)}, bf16[8,256,64]{2,1,0:T(8,128)(2,1)}, bf16[8,256,128]{2,1,0:T(8,128)(2,1)}, f32[256,128]{1,0:T(8,128)}) %tuple.135), branch_computations={%region_1.1_spmd, %region_2.4_spmd} | conditional | flops 25624068 | bytes 496686 | solution.py:99
  115.0 2.1 fusion.6
  117.1 1.7 copy.41
  118.8 7.6 %gather_fusion = f32[2048,128]{1,0:T(8,128)} fusion(f32[2048,128]{1,0:T(8,128)S(1)} %copy-done.1, s32[2048]{0:T(1024)S(1)} %broadcast_clamp_fusion), kind=kCustom, calls=%fused_computation | custom fusion | bytes 2105344 | tf_op jit(solution)/shard_map/gather | solution.py:139
  126.4 2.6 copy.45
  131.5 13.2 %collective-permute-start.7 = (bf16[2048,192]{0,1:T(8,128)(2,1)}, bf16[2048,192]{0,1:T(8,128)(2,1)S(1)}, u32[]{:S(2)}, u32[]{:S(2)}) collective-permute-start(bf16[2048,192]{0,1:T(8,128)(2,1)} %collective-permute-done.6), channel_id=1, source_target_pairs={{1,0},{2,1},{3,2},{4,3},{5,4},{6,5},{7,6},{9,8},{10,9},{11,10},{12... | collective-permute-start | bytes 2359304 | tf_op jit(solution)/shard_map/ppermute | solution.py:12
  144.7 1.9 collective-permute-start.5
  150.0 9.5 %while.51 = (s32[]{:T(128)}, f32[256,128]{1,0:T(8,128)S(1)}, s32[4]{0:T(128)S(1)}, bf16[1,256,64]{2,1,0:T(8,128)(2,1)S(1)}, bf16[4,256,64]{2,1,0:T(8,128)(2,1)},...) while((s32[]{:T(128)}, f32[256,128]{1,0:T(8,128)S(1)}, s32[4]{0:T(128)S(1)}, ...), condition=%wide.region_12.13_spmd, body=%wide.region_7.12_spmd.sunk | while | flops 25624072 | bytes 496837 | solution.py:134
  152.4 2.3 conditional.7
  156.0 2.3 conditional.7
  159.6 2.6 collective-permute-start.8
  162.2 2.2 constant_dynamic-update-slice_fusion.14
  164.3 2.2 constant_dynamic-update-slice_fusion.13
  166.5 2.1 constant_dynamic-update-slice_fusion.12
  169.7 2.1 constant_dynamic-update-slice_fusion.10
  173.9 9.3 %copy.43 = bf16[14336,192]{1,0:T(8,128)(2,1)} copy(bf16[14336,192]{0,1:T(8,128)(2,1)} %constant_dynamic-update-slice_fusion.8) | data formatting | bytes 11010048 | tf_op jit(solution)/shard_map/while | solution.py:83
  184.3 76.1 %while.52 = (s32[]{:T(128)}, f32[2048,128]{1,0:T(8,128)}, s32[]{:T(128)}, s32[8]{0:T(128)S(1)}, bf16[2048,64]{1,0:T(8,128)(2,1)S(1)}, /*index=5*/bf16[14336,192]...) while((s32[]{:T(128)}, f32[2048,128]{1,0:T(8,128)}, ...), condition=%wide.region_18.19_spmd, body=%wide.region_13.18_spmd.sunk | while | flops 1632628736 | bytes 3966781 | solution.py:83
  185.4 9.7 %conditional.8 = (f32[2048,128]{1,0:T(8,128)}) conditional(s32[]{:T(128)} %convert_element_type.117, f32[2048,128]{1,0:T(8,128)} %get-tuple-element.708, (bf16[2048,64]{1,0:T(8,128)(2,1)S(1)}, s32[]{:T(128)}, bf16[14336,192]{1,0:T(8,128)(2,1)}, f32[2048,128]{1,0:T(8,128)}) %tuple.139), branch_computations={%region_14.14_spmd, %region_15.17_spmd} | conditional | flops 1632628736 | bytes 3966534 | solution.py:81
  187.1 8.1 %convolution_add_fusion = f32[2048,128]{1,0:T(8,128)} fusion(f32[2048,128]{1,0:T(8,128)} %get-tuple-element.471, bf16[2048,64]{1,0:T(8,128)(2,1)S(1)} %get-tuple-element.472, f32[2048]{0:T(1024)S(1)} %get-tuple-element.582, f32[2048]{0:T(1024)S(1)} %get-tuple-element.583, bf16[14336,192]{1,0:T(8,128)(2,1)} %get-tuple-element.473, s32[]{:T(128)S(6)} %select_n.56, ...), kind=kOutput, calls=%fused_computation.47 | convolution fusion | flops 1631846400 | bytes 3425792 | tf_op jit(solution)/shard_map/while/body/eval_jaxpr/cond/branch_1_fun/dot_general | solution.py:77
  196.3 9.8 %conditional.8 = (f32[2048,128]{1,0:T(8,128)}) conditional(s32[]{:T(128)} %convert_element_type.117, f32[2048,128]{1,0:T(8,128)} %get-tuple-element.708, (bf16[2048,64]{1,0:T(8,128)(2,1)S(1)}, s32[]{:T(128)}, bf16[14336,192]{1,0:T(8,128)(2,1)}, f32[2048,128]{1,0:T(8,128)}) %tuple.139), branch_computations={%region_14.14_spmd, %region_15.17_spmd} | conditional | flops 1632628736 | bytes 3966534 | solution.py:81
  197.9 8.1 %convolution_add_fusion = f32[2048,128]{1,0:T(8,128)} fusion(f32[2048,128]{1,0:T(8,128)} %get-tuple-element.471, bf16[2048,64]{1,0:T(8,128)(2,1)S(1)} %get-tuple-element.472, f32[2048]{0:T(1024)S(1)} %get-tuple-element.582, f32[2048]{0:T(1024)S(1)} %get-tuple-element.583, bf16[14336,192]{1,0:T(8,128)(2,1)} %get-tuple-element.473, s32[]{:T(128)S(6)} %select_n.56, ...), kind=kOutput, calls=%fused_computation.47 | convolution fusion | flops 1631846400 | bytes 3425792 | tf_op jit(solution)/shard_map/while/body/eval_jaxpr/cond/branch_1_fun/dot_general | solution.py:77
  207.1 9.7 %conditional.8 = (f32[2048,128]{1,0:T(8,128)}) conditional(s32[]{:T(128)} %convert_element_type.117, f32[2048,128]{1,0:T(8,128)} %get-tuple-element.708, (bf16[2048,64]{1,0:T(8,128)(2,1)S(1)}, s32[]{:T(128)}, bf16[14336,192]{1,0:T(8,128)(2,1)}, f32[2048,128]{1,0:T(8,128)}) %tuple.139), branch_computations={%region_14.14_spmd, %region_15.17_spmd} | conditional | flops 1632628736 | bytes 3966534 | solution.py:81
  207.2 1.7 multiply_reduce_fusion.4
  208.8 8.1 %convolution_add_fusion = f32[2048,128]{1,0:T(8,128)} fusion(f32[2048,128]{1,0:T(8,128)} %get-tuple-element.471, bf16[2048,64]{1,0:T(8,128)(2,1)S(1)} %get-tuple-element.472, f32[2048]{0:T(1024)S(1)} %get-tuple-element.582, f32[2048]{0:T(1024)S(1)} %get-tuple-element.583, bf16[14336,192]{1,0:T(8,128)(2,1)} %get-tuple-element.473, s32[]{:T(128)S(6)} %select_n.56, ...), kind=kOutput, calls=%fused_computation.47 | convolution fusion | flops 1631846400 | bytes 3425792 | tf_op jit(solution)/shard_map/while/body/eval_jaxpr/cond/branch_1_fun/dot_general | solution.py:77
  218.0 9.7 %conditional.8 = (f32[2048,128]{1,0:T(8,128)}) conditional(s32[]{:T(128)} %convert_element_type.117, f32[2048,128]{1,0:T(8,128)} %get-tuple-element.708, (bf16[2048,64]{1,0:T(8,128)(2,1)S(1)}, s32[]{:T(128)}, bf16[14336,192]{1,0:T(8,128)(2,1)}, f32[2048,128]{1,0:T(8,128)}) %tuple.139), branch_computations={%region_14.14_spmd, %region_15.17_spmd} | conditional | flops 1632628736 | bytes 3966534 | solution.py:81
  219.7 8.1 %convolution_add_fusion = f32[2048,128]{1,0:T(8,128)} fusion(f32[2048,128]{1,0:T(8,128)} %get-tuple-element.471, bf16[2048,64]{1,0:T(8,128)(2,1)S(1)} %get-tuple-element.472, f32[2048]{0:T(1024)S(1)} %get-tuple-element.582, f32[2048]{0:T(1024)S(1)} %get-tuple-element.583, bf16[14336,192]{1,0:T(8,128)(2,1)} %get-tuple-element.473, s32[]{:T(128)S(6)} %select_n.56, ...), kind=kOutput, calls=%fused_computation.47 | convolution fusion | flops 1631846400 | bytes 3425792 | tf_op jit(solution)/shard_map/while/body/eval_jaxpr/cond/branch_1_fun/dot_general | solution.py:77
  228.9 9.7 %conditional.8 = (f32[2048,128]{1,0:T(8,128)}) conditional(s32[]{:T(128)} %convert_element_type.117, f32[2048,128]{1,0:T(8,128)} %get-tuple-element.708, (bf16[2048,64]{1,0:T(8,128)(2,1)S(1)}, s32[]{:T(128)}, bf16[14336,192]{1,0:T(8,128)(2,1)}, f32[2048,128]{1,0:T(8,128)}) %tuple.139), branch_computations={%region_14.14_spmd, %region_15.17_spmd} | conditional | flops 1632628736 | bytes 3966534 | solution.py:81
  230.5 8.1 %convolution_add_fusion = f32[2048,128]{1,0:T(8,128)} fusion(f32[2048,128]{1,0:T(8,128)} %get-tuple-element.471, bf16[2048,64]{1,0:T(8,128)(2,1)S(1)} %get-tuple-element.472, f32[2048]{0:T(1024)S(1)} %get-tuple-element.582, f32[2048]{0:T(1024)S(1)} %get-tuple-element.583, bf16[14336,192]{1,0:T(8,128)(2,1)} %get-tuple-element.473, s32[]{:T(128)S(6)} %select_n.56, ...), kind=kOutput, calls=%fused_computation.47 | convolution fusion | flops 1631846400 | bytes 3425792 | tf_op jit(solution)/shard_map/while/body/eval_jaxpr/cond/branch_1_fun/dot_general | solution.py:77
  239.7 9.7 %conditional.8 = (f32[2048,128]{1,0:T(8,128)}) conditional(s32[]{:T(128)} %convert_element_type.117, f32[2048,128]{1,0:T(8,128)} %get-tuple-element.708, (bf16[2048,64]{1,0:T(8,128)(2,1)S(1)}, s32[]{:T(128)}, bf16[14336,192]{1,0:T(8,128)(2,1)}, f32[2048,128]{1,0:T(8,128)}) %tuple.139), branch_computations={%region_14.14_spmd, %region_15.17_spmd} | conditional | flops 1632628736 | bytes 3966534 | solution.py:81
  241.4 8.1 %convolution_add_fusion = f32[2048,128]{1,0:T(8,128)} fusion(f32[2048,128]{1,0:T(8,128)} %get-tuple-element.471, bf16[2048,64]{1,0:T(8,128)(2,1)S(1)} %get-tuple-element.472, f32[2048]{0:T(1024)S(1)} %get-tuple-element.582, f32[2048]{0:T(1024)S(1)} %get-tuple-element.583, bf16[14336,192]{1,0:T(8,128)(2,1)} %get-tuple-element.473, s32[]{:T(128)S(6)} %select_n.56, ...), kind=kOutput, calls=%fused_computation.47 | convolution fusion | flops 1631846400 | bytes 3425792 | tf_op jit(solution)/shard_map/while/body/eval_jaxpr/cond/branch_1_fun/dot_general | solution.py:77
  250.6 9.8 %conditional.8 = (f32[2048,128]{1,0:T(8,128)}) conditional(s32[]{:T(128)} %convert_element_type.117, f32[2048,128]{1,0:T(8,128)} %get-tuple-element.708, (bf16[2048,64]{1,0:T(8,128)(2,1)S(1)}, s32[]{:T(128)}, bf16[14336,192]{1,0:T(8,128)(2,1)}, f32[2048,128]{1,0:T(8,128)}) %tuple.139), branch_computations={%region_14.14_spmd, %region_15.17_spmd} | conditional | flops 1632628736 | bytes 3966534 | solution.py:81
  252.3 8.1 %convolution_add_fusion = f32[2048,128]{1,0:T(8,128)} fusion(f32[2048,128]{1,0:T(8,128)} %get-tuple-element.471, bf16[2048,64]{1,0:T(8,128)(2,1)S(1)} %get-tuple-element.472, f32[2048]{0:T(1024)S(1)} %get-tuple-element.582, f32[2048]{0:T(1024)S(1)} %get-tuple-element.583, bf16[14336,192]{1,0:T(8,128)(2,1)} %get-tuple-element.473, s32[]{:T(128)S(6)} %select_n.56, ...), kind=kOutput, calls=%fused_computation.47 | convolution fusion | flops 1631846400 | bytes 3425792 | tf_op jit(solution)/shard_map/while/body/eval_jaxpr/cond/branch_1_fun/dot_general | solution.py:77
  262.0 2.9 %fusion.56 = f32[2048,128]{0,1:T(8,128)} fusion(f32[2048,128]{0,1:T(8,128)S(1)} %copy-done.3, f32[2048,128]{0,1:T(8,128)} %copy.45, f32[2048,128]{0,1:T(8,128)S(1)} %copy.44, bf16[2048,256]{1,0:T(8,128)(2,1)S(1)} %copy-done, f32[256,128]{0,1:T(8,128)S(1)} %copy-done.9, f32[128]{0:T(128)S(1)} %copy-done.15, bf16[1,256,256]{2,1,0:T(8,128)(2,1)S(1)} %copy-done.8, ...), kind=kOutput, calls=%fused_computation.58 | convolution fusion | flops 152141824 | bytes 5636608 | tf_op jit(solution)/shard_map/dot_general | solution.py:138
  264.9 2.5 copy.47
  (110 shorter events, 49.7 us)
Async XLA Ops:
  0.0 10.4 %copy-start = (bf16[2048,256]{1,0:T(8,128)(2,1)S(1)}, bf16[2048,256]{1,0:T(8,128)(2,1)}, u32[]{:S(2)}) copy-start(bf16[2048,256]{1,0:T(8,128)(2,1)} %param.29) | copy-start | bytes 3145732
  0.0 84.9 %copy-start.4 = (bf16[2048,64]{0,1:T(8,128)(2,1)S(1)}, bf16[2048,64]{0,1:T(8,128)(2,1)}, u32[]{:S(2)}) copy-start(bf16[2048,64]{0,1:T(8,128)(2,1)} %param.24) | copy-start | bytes 786436
  0.0 10.9 %copy-start.7 = (bf16[1,256,256]{2,1,0:T(8,128)(2,1)S(1)}, bf16[1,256,256]{2,1,0:T(8,128)(2,1)}, u32[]{:S(2)}) copy-start(bf16[1,256,256]{2,1,0:T(8,128)(2,1)} %param.30) | copy-start | bytes 393220
  0.0 38.1 %copy-start.14 = (s32[1,2048]{1,0:T(1,128)S(1)}, s32[1,2048]{1,0:T(1,128)}, u32[]{:S(2)}) copy-start(s32[1,2048]{1,0:T(1,128)} %param.25) | copy-start | bytes 24580
  0.0 67.9 %copy-start.13 = (bf16[1,256,64]{1,2,0:T(8,128)(2,1)S(1)}, bf16[1,256,64]{1,2,0:T(8,128)(2,1)}, u32[]{:S(2)}) copy-start(bf16[1,256,64]{1,2,0:T(8,128)(2,1)} %param.31) | copy-start | bytes 98308
  1.7 1.0 copy-start.2
  2.7 116.0 %copy-start.1 = (f32[2048,128]{1,0:T(8,128)S(1)}, f32[2048,128]{1,0:T(8,128)}, u32[]{:S(2)}) copy-start(f32[2048,128]{1,0:T(8,128)} %param.27) | copy-start | bytes 3145732
  4.8 33.4 %collective-permute-start.3 = (bf16[2048,192]{0,1:T(8,128)(2,1)}, bf16[2048,192]{0,1:T(8,128)(2,1)}, u32[]{:S(2)}, u32[]{:S(2)}) collective-permute-start(bf16[2048,192]{0,1:T(8,128)(2,1)} %pad_maximum_fusion), channel_id=1, source_target_pairs={{0,1},{1,2},{2,3},{3,4},{4,5},{5,6},{6,7},{8,9},{9,10},{10,11},{11... | collective-permute-start | bytes 2359304 | tf_op jit(solution)/shard_map/ppermute | solution.py:12
  8.5 123.0 %collective-permute-start.6 = (bf16[2048,192]{0,1:T(8,128)(2,1)}, bf16[2048,192]{0,1:T(8,128)(2,1)}, u32[]{:S(2)}, u32[]{:S(2)}) collective-permute-start(bf16[2048,192]{0,1:T(8,128)(2,1)} %pad_maximum_fusion), channel_id=1, source_target_pairs={{1,0},{2,1},{3,2},{4,3},{5,4},{6,5},{7,6},{9,8},{10,9},{11,10},{12... | collective-permute-start | bytes 2359304 | tf_op jit(solution)/shard_map/ppermute | solution.py:12
  37.9 47.3 %copy-start.5 = (bf16[256,128]{0,1:T(8,128)(2,1)}, bf16[256,128]{0,1:T(8,128)(2,1)S(1)}, u32[]{:S(2)}) copy-start(bf16[256,128]{0,1:T(8,128)(2,1)S(1)} %all-reduce.1) | copy-start | bytes 196612
  37.9 24.7 %collective-permute-start = (bf16[1,256,128]{1,2,0:T(8,128)(2,1)S(1)}, bf16[1,256,128]{1,2,0:T(8,128)(2,1)S(1)}, u32[]{:S(2)}, u32[]{:S(2)}) collective-permute-start(bf16[1,256,128]{1,2,0:T(8,128)(2,1)S(1)} %bitcast.116), channel_id=1, source_target_pairs={{0,8},{8,16},{16,24},{24,0},{1,9},{9,17},{17,25},{25,1},{2,10},{10... | collective-permute-start | bytes 196616 | tf_op jit(solution)/shard_map/ppermute | solution.py:115
  38.2 106.5 %collective-permute-start.4 = (bf16[2048,192]{0,1:T(8,128)(2,1)}, bf16[2048,192]{0,1:T(8,128)(2,1)}, u32[]{:S(2)}, u32[]{:S(2)}) collective-permute-start(bf16[2048,192]{0,1:T(8,128)(2,1)} %collective-permute-done.3), channel_id=1, source_target_pairs={{0,1},{1,2},{2,3},{3,4},{4,5},{5,6},{6,7},{8,9},{9,10},{10,11},{11... | collective-permute-start | bytes 2359304 | tf_op jit(solution)/shard_map/ppermute | solution.py:12
  62.6 22.3 %copy-start.12 = (bf16[1,256,128]{1,2,0:T(8,128)(2,1)}, bf16[1,256,128]{1,2,0:T(8,128)(2,1)S(1)}, u32[]{:S(2)}) copy-start(bf16[1,256,128]{1,2,0:T(8,128)(2,1)S(1)} %collective-permute-done) | copy-start | bytes 196612
  62.6 3.2 %collective-permute-start.1 = (bf16[1,256,128]{1,2,0:T(8,128)(2,1)S(1)}, bf16[1,256,128]{1,2,0:T(8,128)(2,1)}, u32[]{:S(2)}, u32[]{:S(2)}) collective-permute-start(bf16[1,256,128]{1,2,0:T(8,128)(2,1)S(1)} %collective-permute-done), channel_id=1, source_target_pairs={{0,8},{8,16},{16,24},{24,0},{1,9},{9,17},{17,25},{25,1},{2,10},{10... | collective-permute-start | bytes 196616 | tf_op jit(solution)/shard_map/ppermute | solution.py:115
  65.8 63.1 %collective-permute-start.2 = (bf16[1,256,128]{1,2,0:T(8,128)(2,1)}, bf16[1,256,128]{1,2,0:T(8,128)(2,1)}, u32[]{:S(2)}, u32[]{:S(2)}) collective-permute-start(bf16[1,256,128]{1,2,0:T(8,128)(2,1)} %collective-permute-done.1), channel_id=1, source_target_pairs={{0,8},{8,16},{16,24},{24,0},{1,9},{9,17},{17,25},{25,1},{2,10},{10... | collective-permute-start | bytes 196616 | tf_op jit(solution)/shard_map/ppermute | solution.py:115
  118.8 27.8 %copy-start.6 = (bf16[256,128]{0,1:T(8,128)(2,1)S(1)}, bf16[256,128]{0,1:T(8,128)(2,1)}, u32[]{:S(2)}) copy-start(bf16[256,128]{0,1:T(8,128)(2,1)} %copy-done.5) | copy-start | bytes 196612
  118.8 31.3 %copy-start.16 = (s32[1,4]{1,0:T(1,128)S(1)}, s32[1,4]{1,0:T(1,128)}, u32[]{:S(2)}) copy-start(s32[1,4]{1,0:T(1,128)} %param.35) | copy-start | bytes 52
  131.5 28.1 %collective-permute-start.7 = (bf16[2048,192]{0,1:T(8,128)(2,1)}, bf16[2048,192]{0,1:T(8,128)(2,1)S(1)}, u32[]{:S(2)}, u32[]{:S(2)}) collective-permute-start(bf16[2048,192]{0,1:T(8,128)(2,1)} %collective-permute-done.6), channel_id=1, source_target_pairs={{1,0},{2,1},{3,2},{4,3},{5,4},{6,5},{7,6},{9,8},{10,9},{11,10},{12... | collective-permute-start | bytes 2359304 | tf_op jit(solution)/shard_map/ppermute | solution.py:12
  144.7 17.5 %collective-permute-start.5 = (bf16[2048,192]{0,1:T(8,128)(2,1)}, bf16[2048,192]{0,1:T(8,128)(2,1)}, u32[]{:S(2)}, u32[]{:S(2)}) collective-permute-start(bf16[2048,192]{0,1:T(8,128)(2,1)} %collective-permute-done.4), channel_id=1, source_target_pairs={{0,1},{1,2},{2,3},{3,4},{4,5},{5,6},{6,7},{8,9},{9,10},{10,11},{11... | collective-permute-start | bytes 2359304 | tf_op jit(solution)/shard_map/ppermute | solution.py:12
  159.5 14.3 %copy-start.10 = (f32[256,128]{1,0:T(8,128)}, f32[256,128]{1,0:T(8,128)S(1)}, u32[]{:S(2)}) copy-start(f32[256,128]{1,0:T(8,128)S(1)} %get-tuple-element.486) | copy-start | bytes 393220
  159.6 13.3 %collective-permute-start.8 = (bf16[2048,192]{0,1:T(8,128)(2,1)S(1)}, bf16[2048,192]{0,1:T(8,128)(2,1)S(1)}, u32[]{:S(2)}, u32[]{:S(2)}) collective-permute-start(bf16[2048,192]{0,1:T(8,128)(2,1)S(1)} %collective-permute-done.7), channel_id=1, source_target_pairs={{1,0},{2,1},{3,2},{4,3},{5,4},{6,5},{7,6},{9,8},{10,9},{11,10},{12... | collective-permute-start | bytes 2359304 | tf_op jit(solution)/shard_map/ppermute | solution.py:12
  173.9 10.4 %copy-start.17 = (s32[1,8]{1,0:T(1,128)S(1)}, s32[1,8]{1,0:T(1,128)}, u32[]{:S(2)}) copy-start(s32[1,8]{1,0:T(1,128)} %param.33) | copy-start | bytes 100
  184.2 77.7 %copy-start.3 = (f32[2048,128]{0,1:T(8,128)S(1)}, f32[2048,128]{0,1:T(8,128)}, u32[]{:S(2)}) copy-start(f32[2048,128]{0,1:T(8,128)} %copy-done.2) | copy-start | bytes 3145732
  184.2 77.7 %copy-start.8 = (bf16[1,256,256]{2,1,0:T(8,128)(2,1)S(1)}, bf16[1,256,256]{2,1,0:T(8,128)(2,1)}, u32[]{:S(2)}) copy-start(bf16[1,256,256]{2,1,0:T(8,128)(2,1)} %param.30) | copy-start | bytes 393220
  184.2 77.7 %copy-start.9 = (f32[256,128]{0,1:T(8,128)S(1)}, f32[256,128]{0,1:T(8,128)}, u32[]{:S(2)}) copy-start(f32[256,128]{0,1:T(8,128)} %copy.41) | copy-start | bytes 393220
  184.2 77.7 %copy-start.11 = (f32[256,128]{1,0:T(8,128)S(1)}, f32[256,128]{1,0:T(8,128)}, u32[]{:S(2)}) copy-start(f32[256,128]{1,0:T(8,128)} %copy-done.10) | copy-start | bytes 393220
  184.2 77.7 %copy-start.15 = (f32[128]{0:T(128)S(1)}, f32[128]{0:T(128)}, u32[]{:S(2)}) copy-start(f32[128]{0:T(128)} %param.28) | copy-start | bytes 1540
